TPU v7x, 128 devices: a whole 4x4x4 slice. The times are simulated.
128 devices in a mesh: rep: 16 (over y, x_lo, core), blk: 8 (over z, x_hi).
Axes of the slice: x: 4 (x_hi: 2, x_lo: 2; x = x_hi * 2 + x_lo), y: 4, z: 4, core: 2. Of those that a mesh axis runs over, the one named last changes fastest.
Arguments:
- tokens: bfloat16 [16384, 1536], P(('rep', 'blk')), may hold values from -64 to 64
- attn_in: float32 [1536, 2048], P(('rep', 'blk')), may hold values from -8 to 8
- attn_out: float32 [1536, 1536], P(('rep', 'blk')), may hold values from -0.15625 to 0.15625
- expert_in: float32 [16, 1536, 1536], P(None, ('rep', 'blk')), may hold values from -0.15625 to 0.15625
- expert_out: float32 [16, 768, 1536], P(None, ('rep', 'blk')), may hold values from -0.21875 to 0.21875
- attn_gain: float32 [1536], replicated, may hold values from 0.25 to 1.75
- moe_gain: float32 [1536], replicated, may hold values from 0.25 to 1.75
- lengths: int32 [16, 6], P('rep'), may hold values from 1 to 512, 1024 in all within a row
- page_table: int32 [16, 8], P('rep'), may hold values from 0 to 7, each once within a row
- routes: int32 [16384, 4], P(('rep', 'blk')), may hold values from 0 to 15, all different within a row; in each aligned block of 128 rows (0 to 127, 128 to 255, ...) at most 64 rows name the same one
- gates: bfloat16 [16384, 4], P(('rep', 'blk')), may hold values from 0.19921875 to 1
Outputs:
- mixed: bfloat16 [16384, 1536], P(('rep', 'blk'))
- kv_cache: bfloat16 [128, 128, 512], P(('rep', 'blk'))
Inputs may be any that keep to these rules, and one draw needn't show every extreme that they name: Each replica's lengths sum to 1024. `page_table`: each replica's row is a permutation of its 8 pages. `routes`: a token names 4 different experts; among the rows of one device no expert is named more than 64 times.
All inputs are finite; a program needn't handle non-finite values.
Results may differ from a plain program's by a relative error of at most 0.013.
Values may be sent and summed in bfloat16 or wider, within the bound.
A program may use at most 128 MiB of HBM per device.

v0:
```python
import functools
import math
import jax
import jax.numpy as jnp
from jax import lax
from jax.sharding import PartitionSpec as P

D = 1536
FF = 768
QH = 12
KVH = 2
HD = 128
E = 16
PAGE = 128
CAP = 64
QW = 1536


def rms_scale(values, gain):
    values = values.astype(jnp.float32)
    mean_sq = jnp.mean(values * values, axis=-1, keepdims=True)
    return values * lax.rsqrt(mean_sq + 1e-06) * gain


def rotate(values, position):
    half = values.shape[-1] // 2
    steps_all = jnp.arange(half, dtype=jnp.float32)
    frequency = jnp.exp(steps_all * (-2.0 * math.log(10000.0) / values.shape[-1]))
    angle = position[:, None] * frequency[None, :]
    cosine = jnp.cos(angle)[:, None, :]
    sine = jnp.sin(angle)[:, None, :]
    front = values[..., :half]
    behind = values[..., half:]
    return jnp.concatenate(
        [front * cosine - behind * sine, behind * cosine + front * sine], axis=-1
    )


def segment_info(lengths, count):
    starts = jnp.cumsum(lengths) - lengths
    index = jnp.arange(count, dtype=jnp.int32)
    member = (index[:, None] >= starts[None, :]).astype(jnp.int32)
    segment = jnp.sum(member, axis=1) - 1
    owner = segment[:, None] == jnp.arange(lengths.shape[0], dtype=jnp.int32)[None, :]
    begin = jnp.sum(jnp.where(owner, starts[None, :], 0), axis=1)
    return (segment, index - begin)


def slot_tables(weight, depth):
    member = (weight > 0).astype(jnp.int32)
    ranked = jnp.cumsum(member, axis=0) - 1
    slot_ids = jnp.arange(depth, dtype=jnp.int32)
    hit = (member.T[:, None, :] == 1) & (ranked.T[:, None, :] == slot_ids[None, :, None])
    onehot = hit.astype(jnp.bfloat16)
    gated = jnp.where(hit, weight.T[:, None, :], jnp.zeros((), jnp.bfloat16))
    return (onehot, gated)


def body(
    tokens,
    attn_in,
    attn_out,
    expert_in,
    expert_out,
    attn_gain,
    moe_gain,
    lengths,
    page_table,
    routes,
    gates,
):
    count = tokens.shape[0]
    cycle_size = lax.axis_size("blk")
    place = lax.axis_index("blk")
    group_rows = count * cycle_size
    local_experts = E // cycle_size
    heads_per = QH // KVH
    segment_all, position_all = segment_info(lengths[0], group_rows)
    first = place * count
    my_index = first + jnp.arange(count, dtype=jnp.int32)
    my_segment = lax.dynamic_slice_in_dim(segment_all, first, count)
    my_position = lax.dynamic_slice_in_dim(position_all, first, count).astype(jnp.float32)
    normed = rms_scale(tokens, attn_gain).astype(jnp.bfloat16)
    columns = normed
    projected = jnp.dot(
        columns,
        lax.all_gather(attn_in.astype(jnp.bfloat16), ("rep", "blk"), axis=0, tiled=True),
        preferred_element_type=jnp.float32,
    )
    queries = rotate(projected[:, :QW].reshape(count, QH, HD), my_position).astype(jnp.bfloat16)
    keys_here = rotate(
        projected[:, QW : QW + KVH * HD].reshape(count, KVH, HD), my_position
    ).astype(jnp.bfloat16)
    values_here = projected[:, QW + KVH * HD :].astype(jnp.bfloat16)
    cache_here = jnp.concatenate([keys_here.reshape(count, KVH * HD), values_here], axis=1)
    cache_all = lax.all_gather(cache_here, "blk", axis=0, tiled=True)
    keys_all = cache_all[:, : KVH * HD].reshape(group_rows, KVH, HD)
    values_all = cache_all[:, KVH * HD :].reshape(group_rows, KVH, HD)
    grouped = queries.reshape(count, KVH, heads_per, HD)
    scores = jnp.einsum(
        "igrd,jgd->grij", grouped, keys_all, preferred_element_type=jnp.float32
    ) / math.sqrt(HD)
    key_index = jnp.arange(group_rows, dtype=jnp.int32)
    allowed = (my_segment[:, None] == segment_all[None, :]) & (
        key_index[None, :] <= my_index[:, None]
    )
    scores = jnp.where(allowed[None, None], scores, jnp.float32(-1e30))
    highest = jnp.max(scores, axis=-1, keepdims=True)
    weights = jnp.exp(scores - highest)
    probs = (weights / jnp.sum(weights, axis=-1, keepdims=True)).astype(jnp.bfloat16)
    attended = jnp.einsum("grij,jgd->igrd", probs, values_all, preferred_element_type=jnp.float32)
    attended = attended.astype(jnp.bfloat16).reshape(count, QW)
    columns = attended
    hidden = tokens.astype(jnp.float32) + jnp.dot(
        columns,
        lax.all_gather(attn_out.astype(jnp.bfloat16), ("rep", "blk"), axis=0, tiled=True),
        preferred_element_type=jnp.float32,
    )
    page_count = count // PAGE
    targets = place * page_count + jnp.arange(page_count, dtype=jnp.int32)
    table = page_table[0]
    logical = jnp.sum(
        jnp.where(
            table[None, :] == targets[:, None],
            jnp.arange(table.shape[0], dtype=jnp.int32)[None, :],
            0,
        ),
        axis=1,
    )
    row_ids = logical[:, None] * PAGE + jnp.arange(PAGE, dtype=jnp.int32)[None, :]
    kv_pages = cache_all[row_ids]
    normed_two = rms_scale(hidden, moe_gain).astype(jnp.bfloat16)
    expert_ids = jnp.arange(E, dtype=jnp.int32)
    dense = jnp.sum(
        jnp.where(
            routes[:, :, None] == expert_ids[None, None, :],
            gates.astype(jnp.float32)[:, :, None],
            jnp.float32(0.0),
        ),
        axis=1,
    ).astype(jnp.bfloat16)
    owned_in, owned_out = (
        lax.all_to_all(
            expert_in.astype(jnp.bfloat16), "blk", split_axis=0, concat_axis=1, tiled=True
        ),
        lax.all_to_all(
            expert_out.astype(jnp.bfloat16), "blk", split_axis=0, concat_axis=1, tiled=True
        ),
    )
    rows_all, weight_all = (
        lax.all_gather(normed_two, "blk", axis=0, tiled=True),
        lax.all_gather(dense, "blk", axis=0, tiled=True),
    )
    owned_weight = lax.dynamic_slice_in_dim(weight_all, place * local_experts, local_experts, 1)
    owned_weight = owned_weight.reshape(cycle_size, count, local_experts)
    onehot, gated = jax.vmap(functools.partial(slot_tables, depth=CAP), in_axes=0, out_axes=1)(
        owned_weight
    )
    chosen = jnp.einsum(
        "jsct,stm->jscm",
        onehot,
        rows_all.reshape(cycle_size, count, D),
        preferred_element_type=jnp.float32,
    ).astype(jnp.bfloat16)
    run_chosen = chosen.reshape(local_experts, cycle_size * CAP, D)
    section = run_chosen
    gate_up = jnp.einsum(
        "erd,edf->erf",
        section,
        lax.all_gather(owned_in, "rep", axis=1, tiled=True),
        preferred_element_type=jnp.float32,
    )
    activated = (jax.nn.relu(gate_up[..., :FF]) * gate_up[..., FF:]).astype(jnp.bfloat16)
    section = activated
    summed = jnp.einsum(
        "erf,efd->erd",
        section,
        lax.all_gather(owned_out, "rep", axis=1, tiled=True),
        preferred_element_type=jnp.float32,
    )
    results = summed.astype(jnp.bfloat16)
    results = results.reshape(local_experts, cycle_size, CAP, D)
    summed = jnp.einsum("jsct,jscm->stm", gated, results, preferred_element_type=jnp.float32)
    expert_term = lax.psum_scatter(
        summed.reshape(count * lax.axis_size("blk"), D).astype(jnp.bfloat16),
        "blk",
        scatter_dimension=0,
        tiled=True,
    ).astype(jnp.float32)
    mixed = (hidden + expert_term).astype(jnp.bfloat16)
    return (mixed, kv_pages)


def solution(mesh):
    in_specs = (
        P(("rep", "blk"), None),
        P(("rep", "blk"), None),
        P(("rep", "blk"), None),
        P(None, ("rep", "blk"), None),
        P(None, ("rep", "blk"), None),
        P(),
        P(),
        P("rep", None),
        P("rep", None),
        P(("rep", "blk"), None),
        P(("rep", "blk"), None),
    )
    out_specs = (P(("rep", "blk"), None), P(("rep", "blk"), None, None))
    return jax.shard_map(body, mesh=mesh, in_specs=in_specs, out_specs=out_specs, check_vma=False)
```

profile of v0, /device:TPU:0, one launch (start us, length us, event | category | flops | bytes accessed | tf_op | source)
XLA Modules:
  0.0 961.2 jit_solution(10468634201662940801)
XLA Ops:
  7.2 1.5 convert_bitcast_fusion
  8.8 1.5 convert_bitcast_fusion.1
  10.4 0.8 reduce-window_clone.1
  12.6 1.2 fusion.12
  13.8 310.3 %all-gather.17.cloned.1.call-done = bf16[128,12,2048]{2,1,0:T(8,128)(2,1)} async-done(((bf16[1,12,2048]{2,1,0:T(8,128)(2,1)}), bf16[128,12,2048]{2,1,0:T(8,128)(2,1)}) %all-gather.17.cloned.1.call-update) | async-done | bytes 6291472 | tf_op jit(solution)/shard_map/all_gather | solution.py:87
  324.1 10.7 %reshape.228 = bf16[1536,2048]{1,0:T(8,128)(2,1)} reshape(bf16[128,12,2048]{2,1,0:T(8,128)(2,1)} %all-gather.17.cloned.1.call-done) | data formatting | bytes 12582912
  334.8 3.8 fusion.28
  339.2 0.7 pad_maximum_fusion.1
  340.3 297.8 %all-gather.19.cloned.1.call-done = bf16[128,12,1536]{2,1,0:T(8,128)(2,1)} async-done(((bf16[1,12,1536]{2,1,0:T(8,128)(2,1)}), bf16[128,12,1536]{2,1,0:T(8,128)(2,1)}) %all-gather.19.cloned.1.call-update) | async-done | bytes 4718608 | tf_op jit(solution)/shard_map/all_gather | solution.py:116
  638.1 8.2 reshape.230
  647.2 42.0 %all-gather.9.cloned.1.call-done = bf16[1024,512]{1,0:T(8,128)(2,1)} async-done(((bf16[128,512]{1,0:T(8,128)(2,1)}), bf16[1024,512]{1,0:T(8,128)(2,1)}) %all-gather.9.cloned.1.call-update) | async-done | bytes 1048592 | tf_op jit(solution)/shard_map/all_gather | solution.py:96
  689.3 1.3 fusion.49
  690.9 4.8 fusion.50
  695.7 3.5 fusion.11
  699.7 0.9 multiply_reduce_fusion
  700.6 0.9 copy-done
  701.5 0.9 multiply_convert_fusion
  702.9 18.1 %all_to_all.36 = bf16[16,12,1536]{2,1,0:T(8,128)(2,1)S(1)} all-to-all(bf16[16,12,1536]{2,1,0:T(8,128)(2,1)S(1)} %copy.101), channel_id=1, replica_groups=mesh['rep'=16,'blk'=8] {'blk'}, dimensions={0} | all-to-all | bytes 1179648 | tf_op jit(solution)/shard_map/all_to_all | solution.py:143
  721.6 0.9 copy.103
  722.8 12.0 %all_to_all.37 = bf16[16,6,1536]{2,1,0:T(8,128)(2,1)S(1)} all-to-all(bf16[16,6,1536]{2,1,0:T(8,128)(2,1)S(1)} %copy.104), channel_id=1, replica_groups=mesh['rep'=16,'blk'=8] {'blk'}, dimensions={0} | all-to-all | bytes 589824 | tf_op jit(solution)/shard_map/all_to_all | solution.py:146
  735.0 0.8 copy.106
  735.9 30.8 %all_gather.24 = bf16[1024,16]{0,1:T(8,128)(2,1)S(1)} all-gather(bf16[128,16]{0,1:T(8,128)(2,1)S(1)} %select_reduce_fusion), channel_id=1, replica_groups=mesh['rep'=16,'blk'=8] {'blk'}, dimensions={0}, use_global_device_ids=true | all-gather | bytes 36864 | tf_op jit(solution)/shard_map/all_gather | solution.py:152
  767.0 23.4 %add_bitcast_fusion = s32[2,8,128]{0,1,2:T(8,128)S(1)} fusion(s32[8,128,2]{2,0,1:T(8,128)S(1)} %copy.97), kind=kOutput, calls=%fused_computation.31 | output fusion | flops 262144 | bytes 16384 | tf_op jit(solution)/shard_map/vmap(jit(cumsum))/reduce_window_sum | solution.py:51
  790.7 2.9 fusion.2
  793.9 28.5 %all-gather.13.cloned.1.call-done = bf16[2,1536,1536]{2,1,0:T(8,128)(2,1)} async-done(((bf16[2,96,1536]{2,1,0:T(8,128)(2,1)}), bf16[2,1536,1536]{2,1,0:T(8,128)(2,1)}) %all-gather.13.cloned.1.call-update) | async-done | bytes 9437200 | tf_op jit(solution)/shard_map/all_gather | solution.py:170
  822.4 10.6 %fusion.55 = f32[2,512,1536]{2,1,0:T(8,128)} fusion(bf16[2,512,1536]{2,1,0:T(8,128)(2,1)S(1)} %bitcast.83, bf16[2,1536,1536]{2,1,0:T(8,128)(2,1)} %all-gather.13.cloned.1.call-done), kind=kOutput, calls=%fused_computation.92 | convolution fusion | flops 4831838208 | bytes 18874368 | tf_op jit(solution)/shard_map/erd,edf->erf/dot_general | solution.py:167
  833.0 30.3 %all-gather.15.cloned.1.call-done = bf16[2,768,1536]{2,1,0:T(8,128)(2,1)} async-done(((bf16[2,48,1536]{2,1,0:T(8,128)(2,1)}), bf16[2,768,1536]{2,1,0:T(8,128)(2,1)}) %all-gather.15.cloned.1.call-update) | async-done | bytes 4718608 | tf_op jit(solution)/shard_map/all_gather | solution.py:178
  863.2 6.8 convolution_convert_fusion
  870.1 2.7 bitcast_convert_fusion
  874.1 1.5 gather_fusion
  875.6 76.9 %reduce-scatter.2.cloned.1.call-done = bf16[128,1536]{1,0:T(8,128)(2,1)} async-done(((bf16[1024,1536]{1,0:T(8,128)(2,1)}), bf16[128,1536]{1,0:T(8,128)(2,1)}) %reduce-scatter.2.cloned.1.call-update) | async-done | bytes 393232 | tf_op jit(solution)/shard_map/reduce_scatter | solution.py:184
  952.5 1.8 add_convert_fusion
  (88 shorter events, 7.2 us)
Async XLA Ops:
  7.2 316.9 %all-gather.17.cloned.1.call-start = ((), (), s32[]{:S(2)}) async-start(), calls=%async_computation.8 | async-start | bytes 8454144 | tf_op jit(solution)/shard_map/all_gather | solution.py:87
  8.8 629.3 %all-gather.19.cloned.1.call-start = ((), (), s32[]{:S(2)}) async-start(), calls=%async_computation.9 | async-start | bytes 6340608 | tf_op jit(solution)/shard_map/all_gather | solution.py:116
  10.4 678.9 %all-gather.9.cloned.1.call-start = ((), (), s32[]{:S(2)}) async-start(), calls=%async_computation.3 | async-start | bytes 1179648 | tf_op jit(solution)/shard_map/all_gather | solution.py:96
  13.8 321.0 %copy-start.3 = (bf16[128,1536]{1,0:T(8,128)(2,1)S(1)}, bf16[128,1536]{1,0:T(8,128)(2,1)}, u32[]{:S(2)}) copy-start(bf16[128,1536]{1,0:T(8,128)(2,1)} %param.11) | copy-start | bytes 1179652
  13.8 321.0 %copy-start.6 = (f32[1536]{0:T(1024)S(1)}, f32[1536]{0:T(1024)}, u32[]{:S(2)}) copy-start(f32[1536]{0:T(1024)} %param.16) | copy-start | bytes 18436
  339.9 450.7 %all-gather.11.cloned.1.call-start = ((), (), s32[]{:S(2)}) async-start(), calls=%async_computation.4 | async-start | bytes 3538944 | tf_op jit(solution)/shard_map/all_gather | solution.py:151
  690.9 8.4 slice-start
  695.7 4.0 slice-start.1
  699.2 2.3 copy-start.7
  699.2 3.2 copy-start.4
  700.6 0.9 copy-start
  701.5 21.1 %copy-start.5 = (f32[16,6,1536]{2,0,1:T(8,128)S(1)}, f32[16,6,1536]{2,0,1:T(8,128)}, u32[]{:S(2)}) copy-start(f32[16,6,1536]{2,0,1:T(8,128)} %param.15) | copy-start | bytes 1769476
  702.4 120.0 %all-gather.13.cloned.1.call-start = ((), (), s32[]{:S(2)}) async-start(), calls=%async_computation.5 | async-start | bytes 10027008 | tf_op jit(solution)/shard_map/all_gather | solution.py:170
  702.5 33.3 %copy-start.9 = (bf16[128,4]{0,1:T(4,128)(2,1)S(1)}, bf16[128,4]{0,1:T(4,128)(2,1)}, u32[]{:S(2)}) copy-start(bf16[128,4]{0,1:T(4,128)(2,1)} %param.21) | copy-start | bytes 3076
  702.6 33.3 %copy-start.8 = (s32[128,4]{0,1:T(4,128)S(1)}, s32[128,4]{0,1:T(4,128)}, u32[]{:S(2)}) copy-start(s32[128,4]{0,1:T(4,128)} %param.20) | copy-start | bytes 6148
  722.5 140.7 %all-gather.15.cloned.1.call-start = ((), (), s32[]{:S(2)}) async-start(), calls=%async_computation.6 | async-start | bytes 5013504 | tf_op jit(solution)/shard_map/all_gather | solution.py:178
  735.8 216.7 %reduce-scatter.2.cloned.1.call-start = ((), (), s32[]{:S(2)}) async-start(), calls=%async_computation.7 | async-start | bytes 3538944 | tf_op jit(solution)/shard_map/reduce_scatter | solution.py:184
  870.1 2.7 copy-start.10
  870.1 4.0 copy-start.2
  870.1 82.4 %copy-start.1 = (f32[128,1536]{1,0:T(8,128)S(1)}, f32[128,1536]{1,0:T(8,128)}, u32[]{:S(2)}) copy-start(f32[128,1536]{1,0:T(8,128)} %copy-done) | copy-start | bytes 2359300
Sparse Core Ops, SparseCore 0:
  10.3 313.7 all-gather.16
  326.3 311.7 all-gather.18
  641.0 48.1 all-gather.8
  702.5 63.4 all-gather.10
  767.5 54.7 all-gather.12
  823.9 39.3 all-gather.14
  872.9 79.5 reduce-scatter.1
where the time goes:
time: 962 us; the launch traced here: 961 us
  waiting for transfers between devices  786 us (82%)
  blocking collectives  60.9 us (6%)
  matrix products  36 us (4%)
  other arithmetic  34.5 us (4%)
  local copies, waits for them, and re-layouts  28.3 us (3%)
  between operations  15.2 us (2%)
    all_gather x1, waiting for transfers between devices, body(): lax.all_gather(attn_in.astype(jnp.bfloat16), ('rep', 'blk'), axis=0, tile...  310 us
    all_gather x1, waiting for transfers between devices, body(): lax.all_gather(attn_out.astype(jnp.bfloat16), ('rep', 'blk'), axis=0, til...  298 us
    reduce_scatter x1, waiting for transfers between devices, body(): lax.psum_scatter(summed.reshape(count * lax.axis_size('blk'), D).astype(j...  76.9 us
    all_gather x1, waiting for transfers between devices, body(): cache_all = lax.all_gather(cache_here, 'blk', axis=0, tiled=True)  42 us
    all_gather x1, blocking collectives, body(): lax.all_gather(dense, 'blk', axis=0, tiled=True)  30.8 us
    all_gather x1, waiting for transfers between devices, body(): lax.all_gather(owned_out, 'rep', axis=1, tiled=True)  30.3 us
    all_gather x1, waiting for transfers between devices, body(): lax.all_gather(owned_in, 'rep', axis=1, tiled=True)  28.5 us
    another operation x1, other arithmetic, slot_tables(): ranked = jnp.cumsum(member, axis=0) - 1  23.4 us
  transfers between devices with their start and end apart: 7, of which 6 were waited for; matrix products, arithmetic and copies ran while one was open for 8% of the time, Pallas kernels for 0%

commit v1 on v0

--- a/solution.py
+++ b/solution.py
@@ -167,7 +167,9 @@
     gate_up = jnp.einsum(
         "erd,edf->erf",
         section,
-        lax.all_gather(owned_in, "rep", axis=1, tiled=True),
+        jnp.concatenate(
+            lax.all_to_all(jnp.stack([owned_in] * lax.axis_size("rep")), "rep", 0, 0), axis=1
+        ),
         preferred_element_type=jnp.float32,
     )
     activated = (jax.nn.relu(gate_up[..., :FF]) * gate_up[..., FF:]).astype(jnp.bfloat16)

time: 962 us -> 1060 us (1.10)
  blocking collectives: 60.9 us -> 158 us
  waiting for transfers between devices: 786 us -> 762 us
  local copies, waits for them, and re-layouts: 28.3 us -> 42.6 us
  starting transfers between devices: 0.29 us -> 12.4 us
    all_gather x1, blocking collectives: 30.8 us -> 158 us  [body(): lax.all_gather(dense, 'blk', axis=0, tiled=True)]
    all_gather x1, waiting for transfers between devices: 30.3 us -> 0.01 us  [body(): lax.all_gather(owned_out, 'rep', axis=1, tiled=True)]
    all_to_all x2 -> x0, blocking collectives: 30.1 us -> none  [the longest x1 18.1 us: body(): lax.all_to_all(expert_in.astype(jnp.bfloat16), 'blk', split_axis=0, conca...]
    all_gather x1 -> x0, waiting for transfers between devices: 28.5 us -> none  [body(): lax.all_gather(owned_in, 'rep', axis=1, tiled=True)]
    all_to_all x0 -> x3, waiting for transfers between devices: none -> 25.2 us  [the longest x1 16.5 us: body(): lax.all_to_all(expert_in.astype(jnp.bfloat16), 'blk', split_axis=0, conca...]
    all_to_all x0 -> x3, starting transfers between devices: none -> 12.1 us  [the longest x1 4.92 us: body(): lax.all_to_all(jnp.stack([owned_in] * lax.axis_size('rep')), 'rep', 0, 0)]
  transfers between devices with their start and end apart: 7 -> 9, of which waited for: 6 -> 6; matrix products, arithmetic and copies ran while one was open for 8% -> 8% of each run, Pallas kernels for 0% -> 0%
where the time goes in v1:
time: 1060 us
  waiting for transfers between devices  762 us (72%)
  blocking collectives  158 us (15%)
  local copies, waits for them, and re-layouts  42.6 us (4%)
  other arithmetic  34.5 us (3%)
  matrix products  32.4 us (3%)
  between operations  15.2 us (1%)
  starting transfers between devices  12.4 us (1%)
    all_gather x1, waiting for transfers between devices, body(): lax.all_gather(attn_in.astype(jnp.bfloat16), ('rep', 'blk'), axis=0, tile...  310 us
    all_gather x1, waiting for transfers between devices, body(): lax.all_gather(attn_out.astype(jnp.bfloat16), ('rep', 'blk'), axis=0, til...  298 us
    all_gather x1, blocking collectives, body(): lax.all_gather(dense, 'blk', axis=0, tiled=True)  158 us
    reduce_scatter x1, waiting for transfers between devices, body(): lax.psum_scatter(summed.reshape(count * lax.axis_size('blk'), D).astype(j...  86.8 us
    all_gather x1, waiting for transfers between devices, body(): cache_all = lax.all_gather(cache_here, 'blk', axis=0, tiled=True)  42.1 us
    another operation x1, other arithmetic, slot_tables(): ranked = jnp.cumsum(member, axis=0) - 1  23.4 us
  transfers between devices with their start and end apart: 9, of which 6 were waited for; matrix products, arithmetic and copies ran while one was open for 8% of the time, Pallas kernels for 0%

profile of v1, /device:TPU:0, one launch (start us, length us, event | category | flops | bytes accessed | tf_op | source)
XLA Modules:
  0.0 1057.5 jit_solution(12842792803762128496)
XLA Ops:
  7.2 1.5 convert_bitcast_fusion
  8.8 1.5 convert_bitcast_fusion.1
  12.6 1.2 fusion.12
  13.8 310.3 %all-gather.14.cloned.1.call-done = bf16[128,12,2048]{2,1,0:T(8,128)(2,1)} async-done(((bf16[1,12,2048]{2,1,0:T(8,128)(2,1)}), bf16[128,12,2048]{2,1,0:T(8,128)(2,1)}) %all-gather.14.cloned.1.call-update) | async-done | bytes 6291472 | tf_op jit(solution)/shard_map/all_gather | solution.py:87
  324.1 10.7 %reshape.239 = bf16[1536,2048]{1,0:T(8,128)(2,1)} reshape(bf16[128,12,2048]{2,1,0:T(8,128)(2,1)} %all-gather.14.cloned.1.call-done) | data formatting | bytes 12582912
  334.8 3.8 fusion.28
  340.3 297.7 %all-gather.16.cloned.1.call-done = bf16[128,12,1536]{2,1,0:T(8,128)(2,1)} async-done(((bf16[1,12,1536]{2,1,0:T(8,128)(2,1)}), bf16[128,12,1536]{2,1,0:T(8,128)(2,1)}) %all-gather.16.cloned.1.call-update) | async-done | bytes 4718608 | tf_op jit(solution)/shard_map/all_gather | solution.py:116
  637.9 8.2 reshape.241
  647.1 42.1 %all-gather.8.cloned.1.call-done = bf16[1024,512]{1,0:T(8,128)(2,1)} async-done(((bf16[128,512]{1,0:T(8,128)(2,1)}), bf16[1024,512]{1,0:T(8,128)(2,1)}) %all-gather.8.cloned.1.call-update) | async-done | bytes 1048592 | tf_op jit(solution)/shard_map/all_gather | solution.py:96
  689.2 1.3 fusion.49
  690.8 4.8 fusion.50
  695.6 3.5 fusion.11
  699.6 0.9 multiply_reduce_fusion
  701.5 1.2 copy.102
  702.8 3.7 all-to-all-start
  706.6 0.9 copy.106
  707.5 16.5 %all-to-all-done = bf16[16,12,1536]{2,1,0:T(8,128)(2,1)S(1)} async-done(((bf16[16,12,1536]{2,1,0:T(8,128)(2,1)}), bf16[16,12,1536]{2,1,0:T(8,128)(2,1)S(1)}, u32[]{:S(2)}, u32[]{:S(2)}) %all-to-all-start) | async-done | bytes 589856 | tf_op jit(solution)/shard_map/all_to_all | solution.py:143
  724.0 3.5 all-to-all-start.2
  728.1 8.7 all-to-all-done.2
  736.8 4.7 stack.5
  741.6 4.9 all-to-all-start.1
  747.6 158.3 %all_gather.21 = bf16[1024,16]{0,1:T(8,128)(2,1)S(1)} all-gather(bf16[128,16]{0,1:T(8,128)(2,1)S(1)} %select_reduce_fusion), channel_id=1, replica_groups=mesh['rep'=16,'blk'=8] {'blk'}, dimensions={0}, use_global_device_ids=true | all-gather | bytes 36864 | tf_op jit(solution)/shard_map/all_gather | solution.py:152
  906.3 23.4 %add_bitcast_fusion = s32[2,8,128]{0,1,2:T(8,128)S(1)} fusion(s32[8,128,2]{2,0,1:T(8,128)S(1)} %copy.98), kind=kOutput, calls=%fused_computation.31 | output fusion | flops 262144 | bytes 16384 | tf_op jit(solution)/shard_map/vmap(jit(cumsum))/reduce_window_sum | solution.py:51
  929.9 8.3 copy.105
  938.2 3.0 fusion.2
  941.5 1.3 copy-done
  942.9 6.9 fusion.55
  949.7 6.8 convolution_convert_fusion
  956.6 2.7 bitcast_convert_fusion
  960.6 1.5 gather_fusion
  962.1 86.8 %reduce-scatter.2.cloned.1.call-done = bf16[128,1536]{1,0:T(8,128)(2,1)} async-done(((bf16[1024,1536]{1,0:T(8,128)(2,1)}), bf16[128,1536]{1,0:T(8,128)(2,1)}) %reduce-scatter.2.cloned.1.call-update) | async-done | bytes 393232 | tf_op jit(solution)/shard_map/reduce_scatter | solution.py:186
  1048.9 1.8 add_convert_fusion
  (89 shorter events, 9.8 us)
Async XLA Ops:
  7.2 316.9 %all-gather.14.cloned.1.call-start = ((), (), s32[]{:S(2)}) async-start(), calls=%async_computation.8 | async-start | bytes 8454144 | tf_op jit(solution)/shard_map/all_gather | solution.py:87
  8.8 629.2 %all-gather.16.cloned.1.call-start = ((), (), s32[]{:S(2)}) async-start(), calls=%async_computation.9 | async-start | bytes 6340608 | tf_op jit(solution)/shard_map/all_gather | solution.py:116
  10.4 678.8 %all-gather.8.cloned.1.call-start = ((), (), s32[]{:S(2)}) async-start(), calls=%async_computation.4 | async-start | bytes 1179648 | tf_op jit(solution)/shard_map/all_gather | solution.py:96
  13.8 321.0 %copy-start.2 = (bf16[128,1536]{1,0:T(8,128)(2,1)S(1)}, bf16[128,1536]{1,0:T(8,128)(2,1)}, u32[]{:S(2)}) copy-start(bf16[128,1536]{1,0:T(8,128)(2,1)} %param.11) | copy-start | bytes 1179652
  13.8 321.0 %copy-start.5 = (f32[1536]{0:T(1024)S(1)}, f32[1536]{0:T(1024)}, u32[]{:S(2)}) copy-start(f32[1536]{0:T(1024)} %param.16) | copy-start | bytes 18436
  339.9 598.3 %all-gather.10.cloned.1.call-start = ((), (), s32[]{:S(2)}) async-start(), calls=%async_computation.5 | async-start | bytes 3538944 | tf_op jit(solution)/shard_map/all_gather | solution.py:151
  690.8 8.4 slice-start
  695.6 4.0 slice-start.1
  699.2 1.4 copy-start.6
  699.2 2.3 copy-start.3
  700.5 6.0 copy-start.4
  702.8 21.2 %all-to-all-start = ((bf16[16,12,1536]{2,1,0:T(8,128)(2,1)}), bf16[16,12,1536]{2,1,0:T(8,128)(2,1)S(1)}, u32[]{:S(2)}, u32[]{:S(2)}) async-start(bf16[16,12,1536]{2,1,0:T(8,128)(2,1)} %copy.102), calls=%async_computation | async-start | bytes 1572864 | tf_op jit(solution)/shard_map/all_to_all | solution.py:143
  724.0 12.9 %all-to-all-start.2 = ((bf16[16,6,1536]{2,1,0:T(8,128)(2,1)}), bf16[16,6,1536]{2,1,0:T(8,128)(2,1)S(1)}, u32[]{:S(2)}, u32[]{:S(2)}) async-start(bf16[16,6,1536]{2,1,0:T(8,128)(2,1)} %copy.106), calls=%async_computation.2 | async-start | bytes 786432 | tf_op jit(solution)/shard_map/all_to_all | solution.py:146
  741.6 6.0 copy-start.8
  741.6 6.1 copy-start.7
  741.6 188.4 %all-to-all-start.1 = ((bf16[16,2,96,1536]{3,2,1,0:T(8,128)(2,1)}), bf16[16,2,96,1536]{3,2,1,0:T(8,128)(2,1)}, u32[]{:S(2)}, u32[]{:S(2)}) async-start(bf16[16,2,96,1536]{3,2,1,0:T(8,128)(2,1)} %stack.5), calls=%async_computation.1 | async-start | bytes 18874368 | tf_op jit(solution)/shard_map/all_to_all | solution.py:171
  746.5 203.3 %all-gather.12.cloned.1.call-start = ((), (), s32[]{:S(2)}) async-start(), calls=%async_computation.6 | async-start | bytes 5013504 | tf_op jit(solution)/shard_map/all_gather | solution.py:180
  747.5 301.3 %reduce-scatter.2.cloned.1.call-start = ((), (), s32[]{:S(2)}) async-start(), calls=%async_computation.7 | async-start | bytes 3538944 | tf_op jit(solution)/shard_map/reduce_scatter | solution.py:186
  938.2 4.6 copy-start
  956.6 2.7 copy-start.9
  956.6 4.0 copy-start.1
Sparse Core Ops, SparseCore 0:
  10.3 313.7 all-gather.13
  326.3 311.5 all-gather.15
  640.9 48.2 all-gather.7
  701.6 72.3 all-gather.9
  776.0 103.3 all-gather.11
  959.4 89.4 reduce-scatter.1
